TPU v7x, 32 devices: a whole 2x2x4 slice. The times are simulated.
32 devices in a mesh: wide: 16 (over z, y, core), shift: 2 (over x).
Axes of the slice: x: 2, y: 2, z: 4, core: 2. Of those that a mesh axis runs over, the one named last changes fastest.
Arguments:
- particles: bfloat16 [1024, 8448], P('wide'), may hold values from -64 to 64
- group_id: int32 [1024, 1], P('wide'), may hold values from 0 to 15; in each aligned block of 64 rows (0 to 63, 64 to 127, ...) at most 8 rows name the same one
- ctf_curves: float32 [16, 4224], P('wide'), may hold values from -1 to 1
- projections: bfloat16 [16, 8448], P('wide')
- inv_noise: float32 [4224], replicated, may hold values from 0.5 to 2
- shifts: int32 [64, 2], P('shift'), may hold values from -8 to 8
Outputs:
- insertion: float32 [16, 12672], P('wide')
- log_evidence: float32 [1024], P('wide')
Inputs may be any that keep to these rules, and one draw needn't show every extreme that they name: `group_id`: at most 8 of the rows of one device name the same group, a bound that some block reaches.
All inputs are finite; a program needn't handle non-finite values.
Results may differ from a plain program's by a relative error of at most 0.0029.
Values may be sent and summed in bfloat16 or wider, within the bound.
A program may use at most 64 MiB of HBM per device.

v0:
```python
import math
import jax
import jax.numpy as jnp
from jax import lax
from jax.sharding import PartitionSpec as P

TWO_PI_BOX = 2.0 * math.pi / 128.0
HIGHEST_PRECISION = lax.Precision.HIGHEST


def shift_tables(shifts, coeffs):
    coeff_index = jnp.arange(coeffs, dtype=jnp.int32)
    freq_x = (coeff_index // 128).astype(jnp.float32)
    freq_y = (coeff_index % 128 - 64).astype(jnp.float32)
    move_x = shifts[:, 0].astype(jnp.float32)
    move_y = shifts[:, 1].astype(jnp.float32)
    phase_angle = TWO_PI_BOX * (
        move_x[:, None] * freq_x[None, :] + move_y[:, None] * freq_y[None, :]
    )
    return (jnp.cos(phase_angle), jnp.sin(phase_angle))


def rotate_slices(slab, cos_table, sin_table):
    coeffs = cos_table.shape[1]
    real_part = slab[:, :coeffs].astype(jnp.float32)[:, None, :]
    imag_part = slab[:, coeffs:].astype(jnp.float32)[:, None, :]
    rot_real = real_part * cos_table[None] + imag_part * sin_table[None]
    rot_imag = imag_part * cos_table[None] - real_part * sin_table[None]
    joined = jnp.concatenate([rot_real, rot_imag], 2)
    return joined.reshape(slab.shape[0] * cos_table.shape[0], 2 * coeffs).astype(jnp.bfloat16)


def slice_scores(weighted, weight_sq, slab, cos_table, sin_table):
    coeffs = cos_table.shape[1]
    n_trans = cos_table.shape[0]
    row_count = weighted.shape[0]
    rotated = rotate_slices(slab, cos_table, sin_table)
    cross_term = lax.dot_general(
        weighted, rotated, (((1,), (1,)), ((), ())), preferred_element_type=jnp.float32
    )
    slice_real = slab[:, :coeffs].astype(jnp.float32)
    slice_imag = slab[:, coeffs:].astype(jnp.float32)
    slice_power = slice_real * slice_real + slice_imag * slice_imag
    self_term = 0.5 * lax.dot_general(
        weight_sq, slice_power, (((1,), (1,)), ((), ())), precision=HIGHEST_PRECISION
    )
    scores = cross_term.reshape(row_count, slab.shape[0], n_trans) - self_term[:, :, None]
    return scores.reshape(row_count, slab.shape[0] * n_trans)


def local(particles, group_id, ctf_curves, projections, inv_noise, shifts):
    coeffs = inv_noise.shape[0]
    n_trans = shifts.shape[0]
    part_rows = particles.shape[0]
    cos_table, sin_table = shift_tables(shifts, coeffs)
    groups = group_id[:, 0]
    gathered_ctf = lax.all_gather(ctf_curves, "wide", axis=0, tiled=True)
    choose_group = (
        groups[:, None] == jnp.arange(gathered_ctf.shape[0], dtype=jnp.int32)[None, :]
    ).astype(jnp.float32)
    ctf_row = jnp.dot(choose_group, gathered_ctf, precision=HIGHEST_PRECISION)
    live_rows = jnp.ones((part_rows,), jnp.float32)
    row_count = particles.shape[0]
    real_part = particles[:, :coeffs].astype(jnp.float32)
    imag_part = particles[:, coeffs:].astype(jnp.float32)
    noise_ctf = inv_noise[None, :] * ctf_row
    weighted = jnp.concatenate([noise_ctf * real_part, noise_ctf * imag_part], 1).astype(
        jnp.bfloat16
    )
    filtered = jnp.concatenate([ctf_row * real_part, ctf_row * imag_part], 1).astype(jnp.bfloat16)
    weight_sq = ctf_row * ctf_row * inv_noise[None, :]
    ctf_square = ctf_row * ctf_row
    slab = lax.all_gather(projections, "wide", axis=0, tiled=True)
    amount = slab.shape[0]
    block_len = math.gcd(amount, 16)
    blocks = slab.reshape(amount // block_len, block_len, slab.shape[1])
    results = lax.map(
        lambda slab_block: slice_scores(weighted, weight_sq, slab_block, cos_table, sin_table),
        blocks,
    )
    scores = jnp.moveaxis(results, 0, 1).reshape(row_count, amount * n_trans)
    local_max = jnp.max(scores, 1)
    row_max = lax.pmax(local_max, "shift")
    row_total = lax.psum(jnp.sum(jnp.exp(scores - row_max[:, None]), 1), "shift")
    weights = (jnp.exp(scores - row_max[:, None]) / row_total[:, None]).astype(jnp.bfloat16)
    log_evidence = row_max + jnp.log(row_total)
    amount = projections.shape[0] * lax.axis_size("wide")
    block_len = math.gcd(amount, 16)

    def one_block(block_id):
        first_orient = block_id * block_len
        weight_block = lax.dynamic_slice_in_dim(
            weights, first_orient * n_trans, block_len * n_trans, 1
        )
        update = lax.dot_general(
            weight_block, filtered, (((0,), (0,)), ((), ())), preferred_element_type=jnp.float32
        )
        update = update.reshape(block_len, n_trans, 2 * coeffs)
        upd_real = update[:, :, :coeffs]
        upd_imag = update[:, :, coeffs:]
        data_real = jnp.sum(upd_real * cos_table[None] - upd_imag * sin_table[None], 1)
        data_imag = jnp.sum(upd_real * sin_table[None] + upd_imag * cos_table[None], 1)
        weight_sum = (
            jnp.sum(weight_block.astype(jnp.float32).reshape(row_count, block_len, n_trans), 2)
            * live_rows[:, None]
        )
        weight_data = lax.dot_general(
            weight_sum, ctf_square, (((0,), (0,)), ((), ())), precision=HIGHEST_PRECISION
        )
        return jnp.concatenate([data_real, data_imag, weight_data], 1)

    results = lax.map(one_block, jnp.arange(amount // block_len, dtype=jnp.int32))
    summed = lax.psum_scatter(
        results.reshape(amount, 3 * coeffs), "wide", scatter_dimension=0, tiled=True
    )
    insertion = lax.psum(summed, "shift")
    return (insertion, log_evidence)


def solution(mesh):
    placed = (
        P("wide", None),
        P("wide", None),
        P("wide", None),
        P("wide", None),
        P(),
        P("shift", None),
    )
    return jax.shard_map(
        local, mesh=mesh, in_specs=placed, out_specs=(P("wide", None), P("wide")), check_vma=False
    )
```

profile of v0, /device:TPU:0, one launch (start us, length us, event | category | flops | bytes accessed | tf_op | source)
XLA Modules:
  0.0 188.0 jit_solution(715756407361464335)
XLA Ops:
  7.2 0.0 all-reduce.3.cloned.1.call-start
  7.2 0.8 convert_bitcast_fusion.1
  8.0 24.1 %all-gather = f32[16,1,4224]{2,1,0:T(1,128)S(1)} all-gather(f32[1,1,4224]{2,1,0:T(1,128)} %bitcast.41), channel_id=1, replica_groups=mesh['wide'=16,'shift'=2] {'wide'}, dimensions={0}, use_global_device_ids=true | all-gather | bytes 287232 | tf_op jit(solution)/shard_map/all_gather | solution.py:57
  32.1 19.1 %all-gather.1 = bf16[16,1,8448]{2,1,0:T(2,128)(2,1)S(1)} all-gather(bf16[1,1,8448]{2,1,0:T(2,128)(2,1)} %bitcast.40), channel_id=1, replica_groups=mesh['wide'=16,'shift'=2] {'wide'}, dimensions={0}, use_global_device_ids=true | all-gather | bytes 287232 | tf_op jit(solution)/shard_map/all_gather | solution.py:73
  51.3 2.1 %fusion.8 = (bf16[64,4224]{1,0:T(8,128)(2,1)S(1)}, bf16[64,4224]{1,0:T(8,128)(2,1)S(1)}, bf16[64,4224]{1,0:T(8,128)(2,1)S(1)}, bf16[64,4224]{1,0:T(8,128)(2,1)S(1)}, f32[64,4224]{1,0:T(8,128)S(1)}) fusion(bf16[64,8448]{1,0:T(8,128)(2,1)} %param.6, f32[4224]{0:T(1024)} %param.10, f32[16,1,4224]{2,1,0:T(1,128)S(1)} %all-gather, s32[64]{0:T(128)} %bitcast.42), kind=kOutput, calls=%fused_computation.15 | convolution fusion | flops 54879232 | bytes 4612864 | tf_op jit(solution)/shard_map/dot_general | solution.py:61
  53.5 1.1 convolution_multiply_fusion
  54.6 2.0 %fusion.21 = (f32[32,4224]{1,0:T(8,128)S(1)}, f32[32,4224]{1,0:T(8,128)S(1)}) fusion(f32[4224]{0:T(1024)S(1)} %get-tuple-element.64, f32[32]{0:T(128)S(1)} %get-tuple-element.59, f32[4224]{0:T(1024)S(1)} %get-tuple-element.63, f32[32]{0:T(128)S(1)} %get-tuple-element.58), kind=kLoop, calls=%fused_computation.32 | loop fusion | flops 540672 | bytes 1115392 | tf_op jit(solution)/shard_map/cos | solution.py:20
  56.6 2.2 %add_convert_fusion = (bf16[16,32,4224]{2,1,0:T(8,128)(2,1)S(1)}, bf16[16,32,4224]{2,1,0:T(8,128)(2,1)S(1)}) fusion(f32[32,4224]{1,0:T(8,128)S(1)} %get-tuple-element.57, f32[16,4224]{1,0:T(8,128)S(1)} %get-tuple-element.48, f32[32,4224]{1,0:T(8,128)S(1)} %get-tuple-element.56, f32[16,4224]{1,0:T(8,128)S(1)} %get-tuple-element.47), kind=kLoop, calls=%fused_computation.7 | loop fusion | flops 17301504 | bytes 10272768 | tf_op jit(solution)/shard_map/convert.2
  58.7 2.4 %fusion.46 = (f32[64]{0:T(128)S(1)}, f32[64,16,32]{0,2,1:T(8,128)S(1)}) fusion(f32[64,16]{0,1:T(8,128)S(1)} %convolution_multiply_fusion, bf16[16,32,4224]{2,1,0:T(8,128)(2,1)S(1)} %get-tuple-element.46, bf16[16,32,4224]{2,1,0:T(8,128)(2,1)S(1)} %get-tuple-element.45, bf16[64,4224]{1,0:T(8,128)(2,1)S(1)} %get-tuple-element.43, ...), kind=kOutput, calls=%fused_computation.73 | convolution fusion | flops 573177792 | bytes 9867520 | tf_op jit(solution)/shard_map/while/body/eval_jaxpr/dot_general | solution.py:38
  61.1 4.9 %pmax.7 = f32[64]{0:T(128)S(1)} all-reduce(f32[64]{0:T(128)S(1)} %get-tuple-element.61), channel_id=1, replica_groups=mesh['wide'=16,'shift'=2] {'shift'}, use_global_device_ids=true, to_apply=%region_1.2 | all-reduce | flops 64 | bytes 512 | tf_op jit(solution)/shard_map/pmax | solution.py:83
  66.1 0.1 fusion.32
  66.2 5.1 %psum.14 = f32[64]{0:T(128)S(1)} all-reduce(f32[64]{0:T(128)S(1)} %fusion.32), channel_id=1, replica_groups=mesh['wide'=16,'shift'=2] {'shift'}, use_global_device_ids=true, to_apply=%region_3.4 | all-reduce | flops 64 | bytes 512 | tf_op jit(solution)/shard_map/psum | solution.py:84
  71.3 0.1 convert_reduce_fusion
  71.3 0.1 fusion.31
  71.4 0.7 fusion.17
  72.1 2.4 %fusion.13 = f32[16,32,8448]{2,1,0:T(8,128)S(1)} fusion(bf16[16,32,64]{2,1,0:T(8,128)(2,1)S(1)} %bitcast.39, bf16[64,4224]{1,0:T(8,128)(2,1)S(1)} %get-tuple-element.42, bf16[64,4224]{1,0:T(8,128)(2,1)S(1)} %get-tuple-element.34), kind=kOutput, calls=%fused_computation.22 | convolution fusion | flops 555810816 | bytes 18448384 | tf_op jit(solution)/shard_map/while/body/eval_jaxpr/dot_general | solution.py:95
  74.5 4.2 %subtract_reduce_fusion = (f32[16,4224]{1,0:T(8,128)S(1)}, f32[16,4224]{1,0:T(8,128)S(1)}) fusion(f32[16,32,8448]{2,1,0:T(8,128)S(1)} %fusion.13, f32[32,4224]{1,0:T(8,128)S(1)} %get-tuple-element.57, f32[32,4224]{1,0:T(8,128)S(1)} %get-tuple-element.56), kind=kLoop, calls=%fused_computation.5 | loop fusion | flops 17166336 | bytes 18923520 | tf_op jit(solution)/shard_map/while/body/eval_jaxpr/reduce_sum | solution.py:101
  78.7 1.0 pad_maximum_fusion
  79.6 0.0 all-reduce.3.cloned.1.call-update
  79.7 0.6 dynamic-slice.1
  80.3 0.5 log_add_fusion
  80.8 89.4 %all-reduce.3.cloned.1.call-done = f32[16,12672]{1,0:T(8,128)} async-done(((f32[16,12672]{1,0:T(8,128)}), f32[16,12672]{1,0:T(8,128)}) %all-reduce.3.cloned.1.call-update) | async-done | bytes 811024
  170.2 1.7 constant_dynamic-slice_fusion
  171.9 9.3 %psum.15 = f32[1,12672]{1,0:T(1,128)} all-reduce(f32[1,12672]{1,0:T(1,128)S(1)} %constant_dynamic-slice_fusion), channel_id=1, replica_groups=mesh['wide'=16,'shift'=2] {'shift'}, use_global_device_ids=true, to_apply=%region_8.9 | all-reduce | flops 12672 | bytes 101376 | tf_op jit(solution)/shard_map/psum | solution.py:116
  (7 shorter events, 0.1 us)
Async XLA Ops:
  7.2 46.3 %copy-start = (f32[4224]{0:T(1024)S(1)}, f32[4224]{0:T(1024)}, u32[]{:S(2)}) copy-start(f32[4224]{0:T(1024)} %param.10) | copy-start | bytes 50692
  7.2 163.0 %all-reduce.3.cloned.1.call-start = ((), (), s32[]{:S(2)}) async-start(), calls=%async_computation | async-start | bytes 1622016
  74.5 5.2 %copy-start.1 = (u32[32]{0:T(128)S(1)}, u32[32]{0:T(128)}, u32[]{:S(2)}) copy-start(u32[32]{0:T(128)} %constant.75) | copy-start | bytes 388
Sparse Core Ops, SparseCore 0:
  79.8 90.3 all-reduce.2
where the time goes:
time: 188 us
  waiting for transfers between devices  89.4 us (48%)
  blocking collectives  62.5 us (33%)
  between operations  14.1 us (8%)
  other arithmetic  10.9 us (6%)
  matrix products  8.68 us (5%)
  local copies, waits for them, and re-layouts  2.31 us (1%)
    unnamed x2, waiting for transfers between devices  89.4 us
    all_gather x1, blocking collectives, local(): gathered_ctf = lax.all_gather(ctf_curves, 'wide', axis=0, tiled=True)  24.1 us
    all_gather x1, blocking collectives, local(): slab = lax.all_gather(projections, 'wide', axis=0, tiled=True)  19.1 us
    psum x1, blocking collectives, local(): insertion = lax.psum(summed, 'shift')  9.26 us
    psum x1, blocking collectives, local(): lax.psum(jnp.sum(jnp.exp(scores - row_max[:, None]), 1), 'shift')  5.1 us
    pmax x1, blocking collectives, local(): row_max = lax.pmax(local_max, 'shift')  4.93 us
    reduce_sum x1, other arithmetic, one_block(): jnp.sum(upd_real * cos_table[None] - upd_imag * sin_table[None], 1)  4.2 us
  transfers between devices with their start and end apart: 1, of which 1 were waited for; matrix products, arithmetic and copies ran while one was open for 1% of the time, Pallas kernels for 0%

commit v1 on v0

--- a/solution.py
+++ b/solution.py
@@ -70,7 +70,23 @@
     filtered = jnp.concatenate([ctf_row * real_part, ctf_row * imag_part], 1).astype(jnp.bfloat16)
     weight_sq = ctf_row * ctf_row * inv_noise[None, :]
     ctf_square = ctf_row * ctf_row
-    slab = lax.all_gather(projections, "wide", axis=0, tiled=True)
+    ways, here, hop = (lax.axis_size("wide"), lax.axis_index("wide"), projections.shape[0])
+    lengths = [n * ways if d == 0 else n for d, n in enumerate(projections.shape)]
+    full = lax.dynamic_update_slice_in_dim(
+        jnp.zeros(lengths, projections.dtype), projections, here * hop, axis=0
+    )
+    going_up = going_down = projections
+    for far in range(1, ways // 2 + 1):
+        going_up = lax.ppermute(going_up, "wide", [(d, (d + 1) % ways) for d in range(ways)])
+        full = lax.dynamic_update_slice_in_dim(full, going_up, (here - far) % ways * hop, axis=0)
+        if 2 * far < ways:
+            going_down = lax.ppermute(
+                going_down, "wide", [(d, (d - 1) % ways) for d in range(ways)]
+            )
+            full = lax.dynamic_update_slice_in_dim(
+                full, going_down, (here + far) % ways * hop, axis=0
+            )
+    slab = full
     amount = slab.shape[0]
     block_len = math.gcd(amount, 16)
     blocks = slab.reshape(amount // block_len, block_len, slab.shape[1])

time: 188 us -> 228 us (1.21)
  starting transfers between devices: 0.04 us -> 28.9 us
  blocking collectives: 62.5 us -> 38.4 us
  local copies, waits for them, and re-layouts: 2.31 us -> 26.1 us
  waiting for transfers between devices: 89.4 us -> 97.8 us
    ppermute x0 -> x15, starting transfers between devices: none -> 28.8 us  [the longest x7 28.3 us: local(): lax.ppermute(going_down, 'wide', [(d, (d - 1) % ways) for d in range(ways)])]
    dynamic_update_slice x0 -> x16, local copies, waits for them, and re-layouts: none -> 23.7 us  [the longest x8 12.2 us: local(): lax.dynamic_update_slice_in_dim(full, going_up, (here - far) % ways * hop...]
    all_gather x1 -> x0, blocking collectives: 19.1 us -> none  [local(): slab = lax.all_gather(projections, 'wide', axis=0, tiled=True)]
    ppermute x0 -> x15, waiting for transfers between devices: none -> 7.5 us  [the longest x8 6.5 us: local(): lax.ppermute(going_up, 'wide', [(d, (d + 1) % ways) for d in range(ways)])]
    all_gather x1, blocking collectives: 24.1 us -> 19.1 us  [local(): gathered_ctf = lax.all_gather(ctf_curves, 'wide', axis=0, tiled=True)]
  transfers between devices with their start and end apart: 1 -> 16, of which waited for: 1 -> 9; matrix products, arithmetic and copies ran while one was open for 1% -> 13% of each run, Pallas kernels for 0% -> 0%
where the time goes in v1:
time: 228 us; the launch traced here: 227 us
  waiting for transfers between devices  97.8 us (43%)
  blocking collectives  38.4 us (17%)
  starting transfers between devices  28.9 us (13%)
  local copies, waits for them, and re-layouts  26.1 us (11%)
  between operations  14.4 us (6%)
  other arithmetic  10.9 us (5%)
  matrix products  10.4 us (5%)
    unnamed x2, waiting for transfers between devices  90.3 us
    ppermute x7, starting transfers between devices, local(): lax.ppermute(going_down, 'wide', [(d, (d - 1) % ways) for d in range(ways)])  28.3 us
    all_gather x1, blocking collectives, local(): gathered_ctf = lax.all_gather(ctf_curves, 'wide', axis=0, tiled=True)  19.1 us
    dynamic_update_slice x8, local copies, waits for them, and re-layouts, local(): lax.dynamic_update_slice_in_dim(full, going_up, (here - far) % ways * hop...  12.2 us
    dynamic_update_slice x7, local copies, waits for them, and re-layouts, local(): lax.dynamic_update_slice_in_dim(full, going_down, (here + far) % ways * h...  10.7 us
    psum x1, blocking collectives, local(): insertion = lax.psum(summed, 'shift')  9.26 us
    ppermute x8, waiting for transfers between devices, local(): lax.ppermute(going_up, 'wide', [(d, (d + 1) % ways) for d in range(ways)])  6.5 us
    psum x1, blocking collectives, local(): lax.psum(jnp.sum(jnp.exp(scores - row_max[:, None]), 1), 'shift')  5.14 us
  transfers between devices with their start and end apart: 16, of which 9 were waited for; matrix products, arithmetic and copies ran while one was open for 13% of the time, Pallas kernels for 0%

profile of v1, /device:TPU:0, one launch (start us, length us, event | category | flops | bytes accessed | tf_op | source)
XLA Modules:
  0.0 226.9 jit_solution(16266990487398225072)
XLA Ops:
  7.8 5.0 %collective-permute-start.1 = (bf16[1,8448]{1,0:T(2,128)(2,1)}, bf16[1,8448]{1,0:T(2,128)(2,1)S(1)}, u32[]{:S(2)}, u32[]{:S(2)}) collective-permute-start(bf16[1,8448]{1,0:T(2,128)(2,1)} %param.9), channel_id=1, source_target_pairs={{0,30},{2,0},{4,2},{6,4},{8,6},{10,8},{12,10},{14,12},{16,14},{18,... | collective-permute-start | bytes 50696 | tf_op jit(solution)/shard_map/ppermute | solution.py:83
  12.8 1.8 collective-permute-done
  14.7 4.3 %collective-permute-start.3 = (bf16[1,8448]{1,0:T(2,128)(2,1)S(1)}, bf16[1,8448]{1,0:T(2,128)(2,1)S(1)}, u32[]{:S(2)}, u32[]{:S(2)}) collective-permute-start(bf16[1,8448]{1,0:T(2,128)(2,1)S(1)} %collective-permute-done.1), channel_id=1, source_target_pairs={{0,30},{2,0},{4,2},{6,4},{8,6},{10,8},{12,10},{14,12},{16,14},{18,... | collective-permute-start | bytes 50696 | tf_op jit(solution)/shard_map/ppermute | solution.py:83
  19.1 1.5 collective-permute-done.2
  20.7 4.4 %collective-permute-start.5 = (bf16[1,8448]{1,0:T(2,128)(2,1)S(1)}, bf16[1,8448]{1,0:T(2,128)(2,1)S(1)}, u32[]{:S(2)}, u32[]{:S(2)}) collective-permute-start(bf16[1,8448]{1,0:T(2,128)(2,1)S(1)} %collective-permute-done.3), channel_id=1, source_target_pairs={{0,30},{2,0},{4,2},{6,4},{8,6},{10,8},{12,10},{14,12},{16,14},{18,... | collective-permute-start | bytes 50696 | tf_op jit(solution)/shard_map/ppermute | solution.py:83
  25.1 1.5 collective-permute-done.4
  27.4 4.5 %collective-permute-start.7 = (bf16[1,8448]{1,0:T(2,128)(2,1)S(1)}, bf16[1,8448]{1,0:T(2,128)(2,1)S(1)}, u32[]{:S(2)}, u32[]{:S(2)}) collective-permute-start(bf16[1,8448]{1,0:T(2,128)(2,1)S(1)} %collective-permute-done.5), channel_id=1, source_target_pairs={{0,30},{2,0},{4,2},{6,4},{8,6},{10,8},{12,10},{14,12},{16,14},{18,... | collective-permute-start | bytes 50696 | tf_op jit(solution)/shard_map/ppermute | solution.py:83
  33.5 4.4 %collective-permute-start.9 = (bf16[1,8448]{1,0:T(2,128)(2,1)S(1)}, bf16[1,8448]{1,0:T(2,128)(2,1)S(1)}, u32[]{:S(2)}, u32[]{:S(2)}) collective-permute-start(bf16[1,8448]{1,0:T(2,128)(2,1)S(1)} %collective-permute-done.7), channel_id=1, source_target_pairs={{0,30},{2,0},{4,2},{6,4},{8,6},{10,8},{12,10},{14,12},{16,14},{18,... | collective-permute-start | bytes 50696 | tf_op jit(solution)/shard_map/ppermute | solution.py:83
  38.9 2.0 fusion.21
  40.9 4.5 %collective-permute-start.11 = (bf16[1,8448]{1,0:T(2,128)(2,1)S(1)}, bf16[1,8448]{1,0:T(2,128)(2,1)}, u32[]{:S(2)}, u32[]{:S(2)}) collective-permute-start(bf16[1,8448]{1,0:T(2,128)(2,1)S(1)} %collective-permute-done.9), channel_id=1, source_target_pairs={{0,30},{2,0},{4,2},{6,4},{8,6},{10,8},{12,10},{14,12},{16,14},{18,... | collective-permute-start | bytes 50696 | tf_op jit(solution)/shard_map/ppermute | solution.py:83
  45.4 19.1 %all-gather = f32[16,1,4224]{2,1,0:T(1,128)S(1)} all-gather(f32[1,1,4224]{2,1,0:T(1,128)} %bitcast.34), channel_id=1, replica_groups=mesh['wide'=16,'shift'=2] {'wide'}, dimensions={0}, use_global_device_ids=true | all-gather | bytes 287232 | tf_op jit(solution)/shard_map/all_gather | solution.py:57
  65.5 3.1 %fusion.8 = (bf16[64,4224]{1,0:T(8,128)(2,1)S(1)}, bf16[64,4224]{1,0:T(8,128)(2,1)S(1)}, bf16[64,4224]{1,0:T(8,128)(2,1)}, bf16[64,4224]{1,0:T(8,128)(2,1)}, f32[64,4224]{1,0:T(8,128)S(1)}) fusion(bf16[64,8448]{1,0:T(8,128)(2,1)} %param.6, f32[4224]{0:T(1024)} %param.10, f32[16,1,4224]{2,1,0:T(1,128)S(1)} %all-gather, s32[64]{0:T(128)} %bitcast.35), kind=kOutput, calls=%fused_computation.15 | convolution fusion | flops 54879232 | bytes 4612864 | tf_op jit(solution)/shard_map/dot_general | solution.py:61
  69.6 1.5 dynamic_update_slice.87
  74.2 1.5 dynamic_update_slice.90
  92.6 1.8 convolution_multiply_fusion
  94.5 2.2 add_convert_fusion
  96.7 2.4 %fusion.46 = (f32[64]{0:T(128)S(1)}, f32[64,16,32]{0,2,1:T(8,128)S(1)}) fusion(f32[64,16]{0,1:T(8,128)S(1)} %convolution_multiply_fusion, bf16[16,32,4224]{2,1,0:T(8,128)(2,1)S(1)} %get-tuple-element.46, bf16[16,32,4224]{2,1,0:T(8,128)(2,1)S(1)} %get-tuple-element.45, bf16[64,4224]{1,0:T(8,128)(2,1)S(1)} %copy-done, bf16[64,4224]{1,0:T(8,128)(2,1)S(1)} %copy-done.1), kind=kOutput, calls=%fused_computation.72 | convolution fusion | flops 573177792 | bytes 9867520 | tf_op jit(solution)/shard_map/while/body/eval_jaxpr/dot_general | solution.py:38
  99.1 4.9 %pmax.7 = f32[64]{0:T(128)S(1)} all-reduce(f32[64]{0:T(128)S(1)} %get-tuple-element.61), channel_id=1, replica_groups=mesh['wide'=16,'shift'=2] {'shift'}, use_global_device_ids=true, to_apply=%region_1.2 | all-reduce | flops 64 | bytes 512 | tf_op jit(solution)/shard_map/pmax | solution.py:99
  104.1 5.1 %psum.14 = f32[64]{0:T(128)S(1)} all-reduce(f32[64]{0:T(128)S(1)} %fusion.32), channel_id=1, replica_groups=mesh['wide'=16,'shift'=2] {'shift'}, use_global_device_ids=true, to_apply=%region_3.4 | all-reduce | flops 64 | bytes 512 | tf_op jit(solution)/shard_map/psum | solution.py:100
  110.0 2.4 %fusion.13 = f32[16,32,8448]{2,1,0:T(8,128)S(1)} fusion(bf16[16,32,64]{2,1,0:T(8,128)(2,1)S(1)} %bitcast.33, bf16[64,4224]{1,0:T(8,128)(2,1)S(1)} %get-tuple-element.42, bf16[64,4224]{1,0:T(8,128)(2,1)S(1)} %get-tuple-element.34), kind=kOutput, calls=%fused_computation.22 | convolution fusion | flops 555810816 | bytes 18448384 | tf_op jit(solution)/shard_map/while/body/eval_jaxpr/dot_general | solution.py:111
  112.4 4.2 %subtract_reduce_fusion = (f32[16,4224]{1,0:T(8,128)S(1)}, f32[16,4224]{1,0:T(8,128)S(1)}) fusion(f32[16,32,8448]{2,1,0:T(8,128)S(1)} %fusion.13, f32[32,4224]{1,0:T(8,128)S(1)} %get-tuple-element.57, f32[32,4224]{1,0:T(8,128)S(1)} %get-tuple-element.56), kind=kLoop, calls=%fused_computation.5 | loop fusion | flops 17166336 | bytes 18923520 | tf_op jit(solution)/shard_map/while/body/eval_jaxpr/reduce_sum | solution.py:117
  118.8 90.3 %all-reduce.3.cloned.1.call-done = f32[16,12672]{1,0:T(8,128)} async-done(((f32[16,12672]{1,0:T(8,128)}), f32[16,12672]{1,0:T(8,128)}) %all-reduce.3.cloned.1.call-update) | async-done | bytes 811024
  209.1 1.7 constant_dynamic-slice_fusion
  210.8 9.3 %psum.15 = f32[1,12672]{1,0:T(1,128)} all-reduce(f32[1,12672]{1,0:T(1,128)S(1)} %constant_dynamic-slice_fusion), channel_id=1, replica_groups=mesh['wide'=16,'shift'=2] {'shift'}, use_global_device_ids=true, to_apply=%region_8.9 | all-reduce | flops 12672 | bytes 101376 | tf_op jit(solution)/shard_map/psum | solution.py:132
  (78 shorter events, 28.8 us)
Async XLA Ops:
  7.2 61.5 %copy-start.2 = (bf16[1,8448]{1,0:T(2,128)(2,1)S(1)}, bf16[1,8448]{1,0:T(2,128)(2,1)}, u32[]{:S(2)}) copy-start(bf16[1,8448]{1,0:T(2,128)(2,1)} %param.9) | copy-start | bytes 50692
  7.2 201.9 %all-reduce.3.cloned.1.call-start = ((), (), s32[]{:S(2)}) async-start(), calls=%async_computation | async-start | bytes 1622016
  7.2 7.3 %collective-permute-start = (bf16[1,8448]{1,0:T(2,128)(2,1)}, bf16[1,8448]{1,0:T(2,128)(2,1)S(1)}, u32[]{:S(2)}, u32[]{:S(2)}) collective-permute-start(bf16[1,8448]{1,0:T(2,128)(2,1)} %param.9), channel_id=1, source_target_pairs={{0,2},{2,4},{4,6},{6,8},{8,10},{10,12},{12,14},{14,16},{16,18},{18... | collective-permute-start | bytes 50696 | tf_op jit(solution)/shard_map/ppermute | solution.py:80
  7.8 7.0 %collective-permute-start.1 = (bf16[1,8448]{1,0:T(2,128)(2,1)}, bf16[1,8448]{1,0:T(2,128)(2,1)S(1)}, u32[]{:S(2)}, u32[]{:S(2)}) collective-permute-start(bf16[1,8448]{1,0:T(2,128)(2,1)} %param.9), channel_id=1, source_target_pairs={{0,30},{2,0},{4,2},{6,4},{8,6},{10,8},{12,10},{14,12},{16,14},{18,... | collective-permute-start | bytes 50696 | tf_op jit(solution)/shard_map/ppermute | solution.py:83
  14.6 24.2 %copy-start.3 = (bf16[1,8448]{1,0:T(2,128)(2,1)}, bf16[1,8448]{1,0:T(2,128)(2,1)S(1)}, u32[]{:S(2)}) copy-start(bf16[1,8448]{1,0:T(2,128)(2,1)S(1)} %collective-permute-done) | copy-start | bytes 50692
  14.6 6.0 %collective-permute-start.2 = (bf16[1,8448]{1,0:T(2,128)(2,1)S(1)}, bf16[1,8448]{1,0:T(2,128)(2,1)S(1)}, u32[]{:S(2)}, u32[]{:S(2)}) collective-permute-start(bf16[1,8448]{1,0:T(2,128)(2,1)S(1)} %collective-permute-done), channel_id=1, source_target_pairs={{0,2},{2,4},{4,6},{6,8},{8,10},{10,12},{12,14},{14,16},{16,18},{18... | collective-permute-start | bytes 50696 | tf_op jit(solution)/shard_map/ppermute | solution.py:80
  14.7 24.1 %copy-start.4 = (bf16[1,8448]{1,0:T(2,128)(2,1)}, bf16[1,8448]{1,0:T(2,128)(2,1)S(1)}, u32[]{:S(2)}) copy-start(bf16[1,8448]{1,0:T(2,128)(2,1)S(1)} %collective-permute-done.1) | copy-start | bytes 50692
  14.7 5.9 %collective-permute-start.3 = (bf16[1,8448]{1,0:T(2,128)(2,1)S(1)}, bf16[1,8448]{1,0:T(2,128)(2,1)S(1)}, u32[]{:S(2)}, u32[]{:S(2)}) collective-permute-start(bf16[1,8448]{1,0:T(2,128)(2,1)S(1)} %collective-permute-done.1), channel_id=1, source_target_pairs={{0,30},{2,0},{4,2},{6,4},{8,6},{10,8},{12,10},{14,12},{16,14},{18,... | collective-permute-start | bytes 50696 | tf_op jit(solution)/shard_map/ppermute | solution.py:83
  20.6 18.2 %copy-start.5 = (bf16[1,8448]{1,0:T(2,128)(2,1)}, bf16[1,8448]{1,0:T(2,128)(2,1)S(1)}, u32[]{:S(2)}) copy-start(bf16[1,8448]{1,0:T(2,128)(2,1)S(1)} %collective-permute-done.2) | copy-start | bytes 50692
  20.6 6.0 %collective-permute-start.4 = (bf16[1,8448]{1,0:T(2,128)(2,1)S(1)}, bf16[1,8448]{1,0:T(2,128)(2,1)S(1)}, u32[]{:S(2)}, u32[]{:S(2)}) collective-permute-start(bf16[1,8448]{1,0:T(2,128)(2,1)S(1)} %collective-permute-done.2), channel_id=1, source_target_pairs={{0,2},{2,4},{4,6},{6,8},{8,10},{10,12},{12,14},{14,16},{16,18},{18... | collective-permute-start | bytes 50696 | tf_op jit(solution)/shard_map/ppermute | solution.py:80
  20.7 6.8 %collective-permute-start.5 = (bf16[1,8448]{1,0:T(2,128)(2,1)S(1)}, bf16[1,8448]{1,0:T(2,128)(2,1)S(1)}, u32[]{:S(2)}, u32[]{:S(2)}) collective-permute-start(bf16[1,8448]{1,0:T(2,128)(2,1)S(1)} %collective-permute-done.3), channel_id=1, source_target_pairs={{0,30},{2,0},{4,2},{6,4},{8,6},{10,8},{12,10},{14,12},{16,14},{18,... | collective-permute-start | bytes 50696 | tf_op jit(solution)/shard_map/ppermute | solution.py:83
  26.7 6.1 %collective-permute-start.6 = (bf16[1,8448]{1,0:T(2,128)(2,1)S(1)}, bf16[1,8448]{1,0:T(2,128)(2,1)S(1)}, u32[]{:S(2)}, u32[]{:S(2)}) collective-permute-start(bf16[1,8448]{1,0:T(2,128)(2,1)S(1)} %collective-permute-done.4), channel_id=1, source_target_pairs={{0,2},{2,4},{4,6},{6,8},{8,10},{10,12},{12,14},{14,16},{16,18},{18... | collective-permute-start | bytes 50696 | tf_op jit(solution)/shard_map/ppermute | solution.py:80
  27.4 6.1 %collective-permute-start.7 = (bf16[1,8448]{1,0:T(2,128)(2,1)S(1)}, bf16[1,8448]{1,0:T(2,128)(2,1)S(1)}, u32[]{:S(2)}, u32[]{:S(2)}) collective-permute-start(bf16[1,8448]{1,0:T(2,128)(2,1)S(1)} %collective-permute-done.5), channel_id=1, source_target_pairs={{0,30},{2,0},{4,2},{6,4},{8,6},{10,8},{12,10},{14,12},{16,14},{18,... | collective-permute-start | bytes 50696 | tf_op jit(solution)/shard_map/ppermute | solution.py:83
  32.8 6.0 %collective-permute-start.8 = (bf16[1,8448]{1,0:T(2,128)(2,1)S(1)}, bf16[1,8448]{1,0:T(2,128)(2,1)S(1)}, u32[]{:S(2)}, u32[]{:S(2)}) collective-permute-start(bf16[1,8448]{1,0:T(2,128)(2,1)S(1)} %collective-permute-done.6), channel_id=1, source_target_pairs={{0,2},{2,4},{4,6},{6,8},{8,10},{10,12},{12,14},{14,16},{16,18},{18... | collective-permute-start | bytes 50696 | tf_op jit(solution)/shard_map/ppermute | solution.py:80
  33.5 32.0 %copy-start.10 = (bf16[1,8448]{1,0:T(2,128)(2,1)}, bf16[1,8448]{1,0:T(2,128)(2,1)S(1)}, u32[]{:S(2)}) copy-start(bf16[1,8448]{1,0:T(2,128)(2,1)S(1)} %collective-permute-done.7) | copy-start | bytes 50692
  33.5 7.3 %collective-permute-start.9 = (bf16[1,8448]{1,0:T(2,128)(2,1)S(1)}, bf16[1,8448]{1,0:T(2,128)(2,1)S(1)}, u32[]{:S(2)}, u32[]{:S(2)}) collective-permute-start(bf16[1,8448]{1,0:T(2,128)(2,1)S(1)} %collective-permute-done.7), channel_id=1, source_target_pairs={{0,30},{2,0},{4,2},{6,4},{8,6},{10,8},{12,10},{14,12},{16,14},{18,... | collective-permute-start | bytes 50696 | tf_op jit(solution)/shard_map/ppermute | solution.py:83
  38.8 26.7 %copy-start.11 = (bf16[1,8448]{1,0:T(2,128)(2,1)}, bf16[1,8448]{1,0:T(2,128)(2,1)S(1)}, u32[]{:S(2)}) copy-start(bf16[1,8448]{1,0:T(2,128)(2,1)S(1)} %collective-permute-done.8) | copy-start | bytes 50692
  38.8 6.6 %collective-permute-start.10 = (bf16[1,8448]{1,0:T(2,128)(2,1)S(1)}, bf16[1,8448]{1,0:T(2,128)(2,1)S(1)}, u32[]{:S(2)}, u32[]{:S(2)}) collective-permute-start(bf16[1,8448]{1,0:T(2,128)(2,1)S(1)} %collective-permute-done.8), channel_id=1, source_target_pairs={{0,2},{2,4},{4,6},{6,8},{8,10},{10,12},{12,14},{14,16},{16,18},{18... | collective-permute-start | bytes 50696 | tf_op jit(solution)/shard_map/ppermute | solution.py:80
  40.9 24.6 %copy-start.12 = (bf16[1,8448]{1,0:T(2,128)(2,1)}, bf16[1,8448]{1,0:T(2,128)(2,1)S(1)}, u32[]{:S(2)}) copy-start(bf16[1,8448]{1,0:T(2,128)(2,1)S(1)} %collective-permute-done.9) | copy-start | bytes 50692
  40.9 23.5 %collective-permute-start.11 = (bf16[1,8448]{1,0:T(2,128)(2,1)S(1)}, bf16[1,8448]{1,0:T(2,128)(2,1)}, u32[]{:S(2)}, u32[]{:S(2)}) collective-permute-start(bf16[1,8448]{1,0:T(2,128)(2,1)S(1)} %collective-permute-done.9), channel_id=1, source_target_pairs={{0,30},{2,0},{4,2},{6,4},{8,6},{10,8},{12,10},{14,12},{16,14},{18,... | collective-permute-start | bytes 50696 | tf_op jit(solution)/shard_map/ppermute | solution.py:83
  45.4 20.2 %copy-start.13 = (bf16[1,8448]{1,0:T(2,128)(2,1)}, bf16[1,8448]{1,0:T(2,128)(2,1)S(1)}, u32[]{:S(2)}) copy-start(bf16[1,8448]{1,0:T(2,128)(2,1)S(1)} %collective-permute-done.10) | copy-start | bytes 50692
  45.4 20.1 %collective-permute-start.12 = (bf16[1,8448]{1,0:T(2,128)(2,1)S(1)}, bf16[1,8448]{1,0:T(2,128)(2,1)}, u32[]{:S(2)}, u32[]{:S(2)}) collective-permute-start(bf16[1,8448]{1,0:T(2,128)(2,1)S(1)} %collective-permute-done.10), channel_id=1, source_target_pairs={{0,2},{2,4},{4,6},{6,8},{8,10},{10,12},{12,14},{14,16},{16,18},{18... | collective-permute-start | bytes 50696 | tf_op jit(solution)/shard_map/ppermute | solution.py:80
  64.4 25.1 %collective-permute-start.13 = (bf16[1,8448]{1,0:T(2,128)(2,1)}, bf16[1,8448]{1,0:T(2,128)(2,1)}, u32[]{:S(2)}, u32[]{:S(2)}) collective-permute-start(bf16[1,8448]{1,0:T(2,128)(2,1)} %collective-permute-done.11), channel_id=1, source_target_pairs={{0,30},{2,0},{4,2},{6,4},{8,6},{10,8},{12,10},{14,12},{16,14},{18,... | collective-permute-start | bytes 50696 | tf_op jit(solution)/shard_map/ppermute | solution.py:83
  65.5 25.6 %collective-permute-start.14 = (bf16[1,8448]{1,0:T(2,128)(2,1)}, bf16[1,8448]{1,0:T(2,128)(2,1)}, u32[]{:S(2)}, u32[]{:S(2)}) collective-permute-start(bf16[1,8448]{1,0:T(2,128)(2,1)} %collective-permute-done.12), channel_id=1, source_target_pairs={{0,2},{2,4},{4,6},{6,8},{8,10},{10,12},{12,14},{14,16},{16,18},{18... | collective-permute-start | bytes 50696 | tf_op jit(solution)/shard_map/ppermute | solution.py:80
  (7 other events, 57.5 us)
Sparse Core Ops, SparseCore 0:
  117.8 91.2 all-reduce.2
